TPU v7x, 512 devices: a whole 4x4x16 slice. The times are simulated.
512 devices in a mesh: dp: 2 (over core), row: 16 (over y, z_lo), col: 16 (over z_hi, x).
Axes of the slice: x: 4, y: 4, z: 16 (z_hi: 4, z_lo: 4; z = z_hi * 4 + z_lo), core: 2. Of those that a mesh axis runs over, the one named last changes fastest.
Arguments:
- queries: bfloat16 [2, 2048, 4096], P('dp', 'row', 'col'), may hold values from -6 to 6
- key_vectors: bfloat16 [2, 2048, 4096], P('dp', 'row', 'col'), may hold values from -6 to 6
- value_vectors: bfloat16 [2, 2048, 4096], P('dp', 'row', 'col'), may hold values from -6 to 6
- out_weight: bfloat16 [4096, 3072], P('row', 'col'), may hold values from -0.09375 to 0.09375
- out_grad: bfloat16 [2, 2048, 3072], P('dp', 'row', 'col'), may hold values from -6 to 6
Outputs:
- output: bfloat16 [2, 2048, 3072], P('dp', 'row', 'col')
- grad_queries: bfloat16 [2, 2048, 4096], P('dp', 'row', 'col')
- grad_keys: bfloat16 [2, 2048, 4096], P('dp', 'row', 'col')
- grad_values: bfloat16 [2, 2048, 4096], P('dp', 'row', 'col')
- grad_weight: float32 [4096, 3072], P(('dp', 'row'), 'col')
All inputs are finite; a program needn't handle non-finite values.
Results may differ from a plain program's by a relative error of at most 0.038.
Values may be sent and summed in bfloat16 or wider, within the bound.
A program may use at most 64 MiB of HBM per device.

v0:
```python
import math
import jax
import jax.numpy as jnp
from jax import lax
from jax.sharding import PartitionSpec as P

HEAD = 128
NEG = -1e30


def split_heads(array_in):
    return array_in.reshape(array_in.shape[0], array_in.shape[1] // HEAD, HEAD)


def merge_heads(array_in):
    return array_in.reshape(array_in.shape[0], array_in.shape[1] * array_in.shape[2])


def causal_scores(query_part, key_part, query_first, key_first):
    scores = jnp.einsum(
        "qhe,khe->qhk", query_part, key_part, preferred_element_type=jnp.float32
    ) * (1.0 / math.sqrt(HEAD))
    query_pos = query_first + lax.broadcasted_iota(jnp.int32, (query_part.shape[0], 1, 1), 0)
    key_pos = key_first + lax.broadcasted_iota(jnp.int32, (1, 1, key_part.shape[0]), 2)
    visible = key_pos <= query_pos
    return (jnp.where(visible, scores, NEG), visible)


def shards(queries, key_vectors, value_vectors, out_weight, out_grad):
    own_rows = queries.shape[1]
    heads_local = queries.shape[2] // HEAD
    own_first = lax.axis_index("row") * own_rows
    own_queries = split_heads(queries[0])
    own_keys = split_heads(key_vectors[0])
    own_values = split_heads(value_vectors[0])
    grad_local = out_grad[0]
    portion = (
        lax.all_gather(key_vectors[0], "row", axis=0, tiled=True),
        lax.all_gather(value_vectors[0], "row", axis=0, tiled=True),
    )
    running_max = jnp.full((own_rows, heads_local), NEG, jnp.float32)
    key_part = split_heads(portion[0])
    value_part = split_heads(portion[1]).astype(jnp.float32)
    scores, visible = causal_scores(own_queries, key_part, own_first, jnp.int32(0))
    new_max = jnp.maximum(running_max, jnp.max(scores, axis=2))
    weights = jnp.where(visible, jnp.exp(scores - new_max[:, :, None]), 0.0)
    running_sum = jnp.sum(weights, axis=2)
    accumulated = jnp.einsum(
        "qhk,khe->qhe",
        weights,
        value_part,
        precision=lax.Precision.HIGHEST,
        preferred_element_type=jnp.float32,
    )
    running_max, running_sum, accumulated = (new_max, running_sum, accumulated)
    attended = merge_heads(accumulated / running_sum[:, :, None]).astype(jnp.bfloat16)
    log_norm = running_max + jnp.log(running_sum)
    attn_full = lax.all_gather(attended, "col", axis=1, tiled=True)
    columns = attn_full
    output_rows = jnp.dot(
        columns,
        lax.all_gather(out_weight, "row", axis=0, tiled=True),
        preferred_element_type=jnp.float32,
    )
    head_terms = lax.dot_general(
        grad_local,
        lax.all_gather(out_weight, "row", axis=0, tiled=True),
        (((1,), (1,)), ((), ())),
        preferred_element_type=jnp.float32,
    )
    grad_attended = lax.psum_scatter(
        head_terms.astype(jnp.bfloat16), "col", scatter_dimension=1, tiled=True
    )
    upstream_own = split_heads(grad_attended)
    row_dot = jnp.sum(
        upstream_own.astype(jnp.float32) * split_heads(attended).astype(jnp.float32), axis=2
    )
    portion = (
        lax.all_gather(key_vectors[0], "row", axis=0, tiled=True),
        lax.all_gather(value_vectors[0], "row", axis=0, tiled=True),
    )
    key_part = split_heads(portion[0])
    value_part = split_heads(portion[1])
    scores, visible = causal_scores(own_queries, key_part, own_first, jnp.int32(0))
    attention = jnp.where(visible, jnp.exp(scores - log_norm[:, :, None]), 0.0)
    grad_probs = jnp.einsum(
        "qhe,khe->qhk", upstream_own, value_part, preferred_element_type=jnp.float32
    )
    grad_scores = (attention * (grad_probs - row_dot[:, :, None])).astype(jnp.bfloat16)
    grad_query_sum = jnp.einsum(
        "qhk,khe->qhe", grad_scores, key_part, preferred_element_type=jnp.float32
    )
    grad_queries = merge_heads(grad_query_sum * (1.0 / math.sqrt(HEAD))).astype(jnp.bfloat16)
    sent = (queries[0].astype(jnp.float32), grad_attended.astype(jnp.float32), log_norm, row_dot)
    portion = (
        lax.all_gather(sent[0], "row", axis=0, tiled=True),
        lax.all_gather(sent[1], "row", axis=0, tiled=True),
        lax.all_gather(sent[2], "row", axis=0, tiled=True),
        lax.all_gather(sent[3], "row", axis=0, tiled=True),
    )
    query_part = split_heads(portion[0].astype(jnp.bfloat16))
    upstream = split_heads(portion[1].astype(jnp.bfloat16))
    norm_part = portion[2]
    dot_part = portion[3]
    scores, visible = causal_scores(query_part, own_keys, jnp.int32(0), own_first)
    attention = jnp.where(visible, jnp.exp(scores - norm_part[:, :, None]), 0.0)
    grad_value_sum = jnp.einsum(
        "qhk,qhe->khe", attention.astype(jnp.bfloat16), upstream, preferred_element_type=jnp.float32
    )
    grad_probs = jnp.einsum(
        "qhe,khe->qhk", upstream, own_values, preferred_element_type=jnp.float32
    )
    grad_scores = (attention * (grad_probs - dot_part[:, :, None])).astype(jnp.bfloat16)
    grad_key_sum = jnp.einsum(
        "qhk,qhe->khe", grad_scores, query_part, preferred_element_type=jnp.float32
    )
    grad_key_sum, grad_value_sum = (grad_key_sum, grad_value_sum)
    grad_keys = merge_heads(grad_key_sum * (1.0 / math.sqrt(HEAD))).astype(jnp.bfloat16)
    grad_values = merge_heads(grad_value_sum).astype(jnp.bfloat16)
    columns = attn_full
    grad_weight = lax.psum_scatter(
        lax.dot_general(
            columns, grad_local, (((0,), (0,)), ((), ())), preferred_element_type=jnp.float32
        ),
        ("dp", "row"),
        scatter_dimension=0,
        tiled=True,
    )
    return (
        output_rows.astype(jnp.bfloat16)[None],
        grad_queries[None],
        grad_keys[None],
        grad_values[None],
        grad_weight,
    )


def solution(mesh):
    return jax.shard_map(
        shards,
        mesh=mesh,
        in_specs=(
            P("dp", "row", "col"),
            P("dp", "row", "col"),
            P("dp", "row", "col"),
            P("row", "col"),
            P("dp", "row", "col"),
        ),
        out_specs=(
            P("dp", "row", "col"),
            P("dp", "row", "col"),
            P("dp", "row", "col"),
            P("dp", "row", "col"),
            P(("dp", "row"), "col"),
        ),
        check_vma=False,
    )
```

profile of v0, /device:TPU:1, one launch (start us, length us, event | category | flops | bytes accessed | tf_op | source)
XLA Modules:
  0.0 794.0 jit_solution(7137687552195433287)
XLA Ops:
  7.2 0.0 all-gather.12.cloned.1.call-start
  7.2 0.7 all-gather.12.cloned.1.call-update
  7.9 0.0 all-gather.18.cloned.1.call-start
  8.0 0.7 all-gather.18.cloned.1.call-update
  8.7 0.0 all-gather.16.cloned.1.call-start
  8.7 1.6 copy.24
  10.3 0.0 all-gather.16.cloned.1.call-update
  10.3 0.0 reduce-scatter.3.cloned.1.call-start
  10.4 78.9 %all-gather.12.cloned.1.call-done = bf16[4096,192]{0,1:T(8,128)(2,1)} async-done(((bf16[256,192]{0,1:T(8,128)(2,1)}), bf16[4096,192]{0,1:T(8,128)(2,1)}) %all-gather.12.cloned.1.call-update) | async-done | bytes 1572880 | tf_op jit(solution)/shard_map/all_gather | solution.py:62
  89.2 2.8 convolution_convert_fusion
  92.1 0.0 reduce-scatter.3.cloned.1.call-update
  92.1 0.0 all-gather.10.cloned.1.call-start
  92.2 0.2 iota_compare_fusion.1
  92.4 85.0 %all-gather.18.cloned.1.call-done = bf16[1,2048,256]{2,1,0:T(8,128)(2,1)} async-done(((bf16[1,128,256]{2,1,0:T(8,128)(2,1)}), bf16[1,2048,256]{2,1,0:T(8,128)(2,1)}) %all-gather.18.cloned.1.call-update) | async-done | bytes 1048592 | tf_op jit(solution)/shard_map/all_gather | solution.py:39
  177.4 1.5 copy.27
  178.9 76.4 %all-gather.16.cloned.1.call-done = bf16[1,2048,256]{1,2,0:T(8,128)(2,1)} async-done(((bf16[1,128,256]{1,2,0:T(8,128)(2,1)}), bf16[1,2048,256]{1,2,0:T(8,128)(2,1)}) %all-gather.16.cloned.1.call-update) | async-done | bytes 1048592 | tf_op jit(solution)/shard_map/all_gather | solution.py:38
  255.2 1.9 fusion.41
  257.1 0.4 fusion.13
  257.6 122.3 %reduce-scatter.3.cloned.1.call-done = bf16[128,256]{1,0:T(8,128)(2,1)} async-done(((bf16[128,4096]{1,0:T(8,128)(2,1)}), bf16[128,256]{1,0:T(8,128)(2,1)}) %reduce-scatter.3.cloned.1.call-update) | async-done | bytes 65552 | tf_op jit(solution)/shard_map/reduce_scatter | solution.py:71
  379.9 1.6 copy.29
  381.4 3.1 multiply_reduce_fusion
  384.6 0.0 all-gather.10.cloned.1.call-update
  384.6 0.0 all-gather.20.cloned.1.call-start
  384.6 0.7 copy.31
  385.4 0.0 all-gather.20.cloned.1.call-update
  385.4 0.0 all-gather.14.cloned.1.call-start
  385.5 0.7 all-gather.14.cloned.1.call-update
  386.2 0.0 reduce-scatter.5.cloned.1.call-start
  386.2 71.2 %all-gather.10.cloned.1.call-done = bf16[128,4096]{0,1:T(8,128)(2,1)} async-done(((bf16[128,256]{0,1:T(8,128)(2,1)}), bf16[128,4096]{0,1:T(8,128)(2,1)}) %all-gather.10.cloned.1.call-update) | async-done | bytes 1048592 | tf_op jit(solution)/shard_map/all_gather | solution.py:58
  457.4 3.4 fusion.36
  460.9 0.8 copy-done.6
  461.7 0.6 reshape_squeeze.10
  462.3 0.1 copy.48
  462.4 0.9 iota_compare_fusion
  463.4 33.1 %all_gather.32 = f32[2048,2]{0,1:T(2,128)S(1)} all-gather(f32[128,2]{0,1:T(2,128)S(1)} %log_add_fusion), channel_id=1, replica_groups=mesh['dp'=2,'row'=16,'col'=16] {'row'}, dimensions={0}, use_global_device_ids=true | all-gather | bytes 17408 | tf_op jit(solution)/shard_map/all_gather | solution.py:98
  496.4 25.6 %all-gather.20.cloned.1.call-done = bf16[1,2048,256]{1,2,0:T(8,128)(2,1)} async-done(((bf16[1,128,256]{1,2,0:T(8,128)(2,1)}), bf16[1,2048,256]{1,2,0:T(8,128)(2,1)}) %all-gather.20.cloned.1.call-update) | async-done | bytes 1048592 | tf_op jit(solution)/shard_map/all_gather | solution.py:96
  522.1 3.6 fusion.8
  525.6 3.0 fusion.21
  528.7 1.7 copy.37
  530.4 35.5 %all_gather.34 = f32[2048,2]{0,1:T(2,128)S(1)} all-gather(f32[128,2]{0,1:T(2,128)S(1)} %get-tuple-element.17), channel_id=1, replica_groups=mesh['dp'=2,'row'=16,'col'=16] {'row'}, dimensions={0}, use_global_device_ids=true | all-gather | bytes 17408 | tf_op jit(solution)/shard_map/all_gather | solution.py:99
  565.9 44.3 %all-gather.14.cloned.1.call-done = bf16[2048,256]{1,0:T(8,128)(2,1)} async-done(((bf16[128,256]{1,0:T(8,128)(2,1)}), bf16[2048,256]{1,0:T(8,128)(2,1)}) %all-gather.14.cloned.1.call-update) | async-done | bytes 1048592 | tf_op jit(solution)/shard_map/all_gather | solution.py:97
  610.2 1.5 copy.49
  611.7 2.0 fusion.23
  613.7 0.7 copy.38
  614.4 0.4 convolution_convert_fusion.1
  614.9 0.7 copy.39
  615.6 2.9 fusion.24
  618.5 168.6 %reduce-scatter.5.cloned.1.call-done = f32[128,192]{0,1:T(8,128)} async-done(((f32[4096,192]{0,1:T(8,128)}), f32[128,192]{0,1:T(8,128)}) %reduce-scatter.5.cloned.1.call-update) | async-done | bytes 98320 | tf_op jit(solution)/shard_map/reduce_scatter | solution.py:121
  (20 shorter events, 0.1 us)
Async XLA Ops:
  7.2 82.1 %copy-start = (bf16[1,128,192]{1,2,0:T(8,128)(2,1)S(1)}, bf16[1,128,192]{1,2,0:T(8,128)(2,1)}, u32[]{:S(2)}) copy-start(bf16[1,128,192]{1,2,0:T(8,128)(2,1)} %param.9) | copy-start | bytes 147460
  7.2 85.0 %copy-start.4 = (bf16[1,128,256]{2,1,0:T(8,128)(2,1)S(1)}, bf16[1,128,256]{2,1,0:T(8,128)(2,1)}, u32[]{:S(2)}) copy-start(bf16[1,128,256]{2,1,0:T(8,128)(2,1)} %param.5) | copy-start | bytes 196612
  7.2 82.0 %all-gather.12.cloned.1.call-start = ((), (), s32[]{:S(2)}) async-start(), calls=%async_computation.3 | async-start | bytes 1671168 | tf_op jit(solution)/shard_map/all_gather | solution.py:62
  7.9 169.4 %all-gather.18.cloned.1.call-start = ((), (), s32[]{:S(2)}) async-start(), calls=%async_computation.8 | async-start | bytes 1114112 | tf_op jit(solution)/shard_map/all_gather | solution.py:39
  8.7 246.6 %all-gather.16.cloned.1.call-start = ((), (), s32[]{:S(2)}) async-start(), calls=%async_computation.7 | async-start | bytes 1114112 | tf_op jit(solution)/shard_map/all_gather | solution.py:38
  10.3 369.5 %reduce-scatter.3.cloned.1.call-start = ((), (), s32[]{:S(2)}) async-start(), calls=%async_computation.4 | async-start | bytes 1114112 | tf_op jit(solution)/shard_map/reduce_scatter | solution.py:71
  92.1 365.3 %all-gather.10.cloned.1.call-start = ((), (), s32[]{:S(2)}) async-start(), calls=%async_computation.2 | async-start | bytes 1114112 | tf_op jit(solution)/shard_map/all_gather | solution.py:58
  178.9 202.6 %copy-start.3 = (bf16[1,2048,256]{1,2,0:T(8,128)(2,1)}, bf16[1,2048,256]{1,2,0:T(8,128)(2,1)S(1)}, u32[]{:S(2)}) copy-start(bf16[1,2048,256]{1,2,0:T(8,128)(2,1)S(1)} %copy.27) | copy-start | bytes 3145732
  381.4 3.2 copy-start.5
  384.6 137.5 %all-gather.20.cloned.1.call-start = ((), (), s32[]{:S(2)}) async-start(), calls=%async_computation.9 | async-start | bytes 1114112 | tf_op jit(solution)/shard_map/all_gather | solution.py:96
  385.4 224.8 %all-gather.14.cloned.1.call-start = ((), (), s32[]{:S(2)}) async-start(), calls=%async_computation.5 | async-start | bytes 1114112 | tf_op jit(solution)/shard_map/all_gather | solution.py:97
  386.2 401.0 %reduce-scatter.5.cloned.1.call-start = ((), (), s32[]{:S(2)}) async-start(), calls=%async_computation.6 | async-start | bytes 3244032 | tf_op jit(solution)/shard_map/reduce_scatter | solution.py:121
  460.8 0.8 copy-start.6
  460.8 1.5 copy-start.7
  522.1 3.6 copy-start.2
  528.7 83.0 %copy-start.1 = (f32[2048,2,128]{0,2,1:T(8,128)S(1)}, f32[2048,2,128]{0,2,1:T(8,128)}, u32[]{:S(2)}) copy-start(f32[2048,2,128]{0,2,1:T(8,128)} %fusion.8) | copy-start | bytes 6291460
Sparse Core Ops, SparseCore 0:
  10.0 79.1 all-gather.11
  91.3 86.0 all-gather.17
  179.9 75.2 all-gather.15
  259.2 120.6 reduce-scatter.2
  384.7 72.6 all-gather.9
  460.0 61.9 all-gather.19
  524.4 85.7 all-gather.13
  613.8 173.2 reduce-scatter.4
where the time goes:
time: 795 us; the launch traced here: 794 us
  waiting for transfers between devices  674 us (85%)
  blocking collectives  68.5 us (9%)
  matrix products  23.2 us (3%)
  between operations  14.3 us (2%)
  local copies, waits for them, and re-layouts  11.7 us (1%)
    reduce_scatter x1, waiting for transfers between devices, shards(): lax.psum_scatter(lax.dot_general(columns, grad_local, (((0,), (0,)), ((),...  169 us
    reduce_scatter x1, waiting for transfers between devices, shards(): lax.psum_scatter(head_terms.astype(jnp.bfloat16), 'col', scatter_dimensio...  122 us
    all_gather x1, waiting for transfers between devices, shards(): lax.all_gather(value_vectors[0], 'row', axis=0, tiled=True)  85 us
    all_gather x1, waiting for transfers between devices, shards(): lax.all_gather(out_weight, 'row', axis=0, tiled=True)  78.9 us
    all_gather x1, waiting for transfers between devices, shards(): lax.all_gather(key_vectors[0], 'row', axis=0, tiled=True)  76.4 us
    all_gather x1, waiting for transfers between devices, shards(): attn_full = lax.all_gather(attended, 'col', axis=1, tiled=True)  71.2 us
    all_gather x1, waiting for transfers between devices, shards(): lax.all_gather(sent[1], 'row', axis=0, tiled=True)  44.3 us
    all_gather x1, blocking collectives, shards(): lax.all_gather(sent[3], 'row', axis=0, tiled=True)  35.5 us
  transfers between devices with their start and end apart: 8, of which 8 were waited for; matrix products, arithmetic and copies ran while one was open for 4% of the time, Pallas kernels for 0%

commit v1 on v0

--- a/solution.py
+++ b/solution.py
@@ -3,6 +3,7 @@
 import jax.numpy as jnp
 from jax import lax
 from jax.sharding import PartitionSpec as P
+from jax.lax import all_to_all, axis_size
 
 HEAD = 128
 NEG = -1e30
@@ -96,7 +97,7 @@
         lax.all_gather(sent[0], "row", axis=0, tiled=True),
         lax.all_gather(sent[1], "row", axis=0, tiled=True),
         lax.all_gather(sent[2], "row", axis=0, tiled=True),
-        lax.all_gather(sent[3], "row", axis=0, tiled=True),
+        jnp.concatenate(all_to_all(jnp.stack(axis_size("row") * [sent[3]]), "row", 0, 0), 0),
     )
     query_part = split_heads(portion[0].astype(jnp.bfloat16))
     upstream = split_heads(portion[1].astype(jnp.bfloat16))

time: 795 us -> 794 us (level)
  blocking collectives: 68.5 us -> 33.3 us
  waiting for transfers between devices: 674 us -> 702 us
    all_gather x1 -> x0, blocking collectives: 35.5 us -> none  [shards(): lax.all_gather(sent[3], 'row', axis=0, tiled=True)]
    all_gather x1, waiting for transfers between devices: 44.3 us -> 71.8 us  [shards(): lax.all_gather(sent[1], 'row', axis=0, tiled=True)]
  transfers between devices with their start and end apart: 8 -> 9, of which waited for: 8 -> 8; matrix products, arithmetic and copies ran while one was open for 4% -> 4% of each run, Pallas kernels for 0% -> 0%
where the time goes in v1:
time: 794 us; the launch traced here: 793 us
  waiting for transfers between devices  702 us (88%)
  blocking collectives  33.3 us (4%)
  matrix products  23.1 us (3%)
  between operations  14.3 us (2%)
  local copies, waits for them, and re-layouts  12.2 us (2%)
    reduce_scatter x1, waiting for transfers between devices, shards(): lax.psum_scatter(lax.dot_general(columns, grad_local, (((0,), (0,)), ((),...  168 us
    reduce_scatter x1, waiting for transfers between devices, shards(): lax.psum_scatter(head_terms.astype(jnp.bfloat16), 'col', scatter_dimensio...  122 us
    all_gather x1, waiting for transfers between devices, shards(): lax.all_gather(value_vectors[0], 'row', axis=0, tiled=True)  85 us
    all_gather x1, waiting for transfers between devices, shards(): lax.all_gather(out_weight, 'row', axis=0, tiled=True)  78.9 us
    all_gather x1, waiting for transfers between devices, shards(): lax.all_gather(key_vectors[0], 'row', axis=0, tiled=True)  76.4 us
    all_gather x1, waiting for transfers between devices, shards(): lax.all_gather(sent[1], 'row', axis=0, tiled=True)  71.8 us
    all_gather x1, waiting for transfers between devices, shards(): attn_full = lax.all_gather(attended, 'col', axis=1, tiled=True)  71.2 us
    all_gather x1, blocking collectives, shards(): lax.all_gather(sent[2], 'row', axis=0, tiled=True)  33.3 us
  transfers between devices with their start and end apart: 9, of which 8 were waited for; matrix products, arithmetic and copies ran while one was open for 4% of the time, Pallas kernels for 0%

profile of v1, /device:TPU:1, one launch (start us, length us, event | category | flops | bytes accessed | tf_op | source)
XLA Modules:
  0.0 793.3 jit_solution(5351877498228340934)
XLA Ops:
  7.2 0.0 all-gather.12.cloned.1.call-start
  7.2 0.7 all-gather.12.cloned.1.call-update
  7.9 0.0 all-gather.18.cloned.1.call-start
  8.0 0.7 all-gather.18.cloned.1.call-update
  8.7 0.0 all-gather.16.cloned.1.call-start
  8.7 1.6 copy.40
  10.3 0.0 all-gather.16.cloned.1.call-update
  10.3 0.0 reduce-scatter.3.cloned.1.call-start
  10.4 78.9 %all-gather.12.cloned.1.call-done = bf16[4096,192]{0,1:T(8,128)(2,1)} async-done(((bf16[256,192]{0,1:T(8,128)(2,1)}), bf16[4096,192]{0,1:T(8,128)(2,1)}) %all-gather.12.cloned.1.call-update) | async-done | bytes 1572880 | tf_op jit(solution)/shard_map/all_gather | solution.py:63
  89.2 2.8 convolution_convert_fusion
  92.1 0.0 reduce-scatter.3.cloned.1.call-update
  92.1 0.0 all-gather.10.cloned.1.call-start
  92.2 0.2 iota_compare_fusion.1
  92.4 85.0 %all-gather.18.cloned.1.call-done = bf16[1,2048,256]{2,1,0:T(8,128)(2,1)} async-done(((bf16[1,128,256]{2,1,0:T(8,128)(2,1)}), bf16[1,2048,256]{2,1,0:T(8,128)(2,1)}) %all-gather.18.cloned.1.call-update) | async-done | bytes 1048592 | tf_op jit(solution)/shard_map/all_gather | solution.py:40
  177.4 1.5 copy.43
  178.9 76.4 %all-gather.16.cloned.1.call-done = bf16[1,2048,256]{1,2,0:T(8,128)(2,1)} async-done(((bf16[1,128,256]{1,2,0:T(8,128)(2,1)}), bf16[1,2048,256]{1,2,0:T(8,128)(2,1)}) %all-gather.16.cloned.1.call-update) | async-done | bytes 1048592 | tf_op jit(solution)/shard_map/all_gather | solution.py:39
  255.2 1.9 fusion.43
  257.1 0.4 fusion.13
  257.6 122.3 %reduce-scatter.3.cloned.1.call-done = bf16[128,256]{1,0:T(8,128)(2,1)} async-done(((bf16[128,4096]{1,0:T(8,128)(2,1)}), bf16[128,256]{1,0:T(8,128)(2,1)}) %reduce-scatter.3.cloned.1.call-update) | async-done | bytes 65552 | tf_op jit(solution)/shard_map/reduce_scatter | solution.py:72
  379.9 1.6 copy.45
  381.4 3.1 multiply_reduce_fusion
  384.6 0.0 all-gather.10.cloned.1.call-update
  384.6 0.0 all-gather.20.cloned.1.call-start
  384.6 0.7 copy.50
  385.4 0.0 all-gather.20.cloned.1.call-update
  385.4 0.0 all-gather.14.cloned.1.call-start
  385.5 0.7 all-gather.14.cloned.1.call-update
  386.2 0.0 reduce-scatter.5.cloned.1.call-start
  386.2 71.2 %all-gather.10.cloned.1.call-done = bf16[128,4096]{0,1:T(8,128)(2,1)} async-done(((bf16[128,256]{0,1:T(8,128)(2,1)}), bf16[128,4096]{0,1:T(8,128)(2,1)}) %all-gather.10.cloned.1.call-update) | async-done | bytes 1048592 | tf_op jit(solution)/shard_map/all_gather | solution.py:59
  457.4 3.4 fusion.38
  460.9 0.8 copy-done.6
  461.7 0.6 reshape_squeeze.10
  462.4 0.9 iota_compare_fusion
  463.3 33.3 %all_gather.29 = f32[2048,2]{0,1:T(2,128)S(1)} all-gather(f32[128,2]{0,1:T(2,128)S(1)} %log_add_fusion), channel_id=1, replica_groups=mesh['dp'=2,'row'=16,'col'=16] {'row'}, dimensions={0}, use_global_device_ids=true | all-gather | bytes 17408 | tf_op jit(solution)/shard_map/all_gather | solution.py:99
  496.6 25.7 %all-gather.20.cloned.1.call-done = bf16[1,2048,256]{1,2,0:T(8,128)(2,1)} async-done(((bf16[1,128,256]{1,2,0:T(8,128)(2,1)}), bf16[1,2048,256]{1,2,0:T(8,128)(2,1)}) %all-gather.20.cloned.1.call-update) | async-done | bytes 1048592 | tf_op jit(solution)/shard_map/all_gather | solution.py:97
  522.3 3.6 fusion.8
  525.8 0.6 stack.2
  526.5 6.9 all-to-all-start
  533.4 3.0 fusion.21
  536.4 1.7 copy.59
  538.2 71.8 %all-gather.14.cloned.1.call-done = bf16[2048,256]{1,0:T(8,128)(2,1)} async-done(((bf16[128,256]{1,0:T(8,128)(2,1)}), bf16[2048,256]{1,0:T(8,128)(2,1)}) %all-gather.14.cloned.1.call-update) | async-done | bytes 1048592 | tf_op jit(solution)/shard_map/all_gather | solution.py:98
  609.9 1.5 copy.72
  611.4 1.9 fusion.23
  613.4 0.7 copy.60
  614.1 0.4 convolution_convert_fusion.1
  614.6 0.7 copy.61
  615.3 2.9 fusion.24
  618.2 168.3 %reduce-scatter.5.cloned.1.call-done = f32[128,192]{0,1:T(8,128)} async-done(((f32[4096,192]{0,1:T(8,128)}), f32[128,192]{0,1:T(8,128)}) %reduce-scatter.5.cloned.1.call-update) | async-done | bytes 98320 | tf_op jit(solution)/shard_map/reduce_scatter | solution.py:122
  (22 shorter events, 0.1 us)
Async XLA Ops:
  7.2 82.1 %copy-start = (bf16[1,128,192]{1,2,0:T(8,128)(2,1)S(1)}, bf16[1,128,192]{1,2,0:T(8,128)(2,1)}, u32[]{:S(2)}) copy-start(bf16[1,128,192]{1,2,0:T(8,128)(2,1)} %param.9) | copy-start | bytes 147460
  7.2 85.0 %copy-start.4 = (bf16[1,128,256]{2,1,0:T(8,128)(2,1)S(1)}, bf16[1,128,256]{2,1,0:T(8,128)(2,1)}, u32[]{:S(2)}) copy-start(bf16[1,128,256]{2,1,0:T(8,128)(2,1)} %param.5) | copy-start | bytes 196612
  7.2 82.0 %all-gather.12.cloned.1.call-start = ((), (), s32[]{:S(2)}) async-start(), calls=%async_computation.4 | async-start | bytes 1671168 | tf_op jit(solution)/shard_map/all_gather | solution.py:63
  7.9 169.4 %all-gather.18.cloned.1.call-start = ((), (), s32[]{:S(2)}) async-start(), calls=%async_computation.9 | async-start | bytes 1114112 | tf_op jit(solution)/shard_map/all_gather | solution.py:40
  8.7 246.6 %all-gather.16.cloned.1.call-start = ((), (), s32[]{:S(2)}) async-start(), calls=%async_computation.8 | async-start | bytes 1114112 | tf_op jit(solution)/shard_map/all_gather | solution.py:39
  10.3 369.5 %reduce-scatter.3.cloned.1.call-start = ((), (), s32[]{:S(2)}) async-start(), calls=%async_computation.5 | async-start | bytes 1114112 | tf_op jit(solution)/shard_map/reduce_scatter | solution.py:72
  92.1 365.3 %all-gather.10.cloned.1.call-start = ((), (), s32[]{:S(2)}) async-start(), calls=%async_computation.3 | async-start | bytes 1114112 | tf_op jit(solution)/shard_map/all_gather | solution.py:59
  178.9 202.6 %copy-start.3 = (bf16[1,2048,256]{1,2,0:T(8,128)(2,1)}, bf16[1,2048,256]{1,2,0:T(8,128)(2,1)S(1)}, u32[]{:S(2)}) copy-start(bf16[1,2048,256]{1,2,0:T(8,128)(2,1)S(1)} %copy.43) | copy-start | bytes 3145732
  381.4 3.2 copy-start.5
  384.6 137.7 %all-gather.20.cloned.1.call-start = ((), (), s32[]{:S(2)}) async-start(), calls=%async_computation.10 | async-start | bytes 1114112 | tf_op jit(solution)/shard_map/all_gather | solution.py:97
  385.4 224.5 %all-gather.14.cloned.1.call-start = ((), (), s32[]{:S(2)}) async-start(), calls=%async_computation.6 | async-start | bytes 1114112 | tf_op jit(solution)/shard_map/all_gather | solution.py:98
  386.2 400.3 %reduce-scatter.5.cloned.1.call-start = ((), (), s32[]{:S(2)}) async-start(), calls=%async_computation.7 | async-start | bytes 3244032 | tf_op jit(solution)/shard_map/reduce_scatter | solution.py:122
  460.8 0.8 copy-start.6
  460.8 1.5 copy-start.7
  522.3 11.1 %copy-start.2 = (bf16[1,2048,256]{1,2,0:T(8,128)(2,1)S(1)}, bf16[1,2048,256]{1,2,0:T(8,128)(2,1)}, u32[]{:S(2)}) copy-start(bf16[1,2048,256]{1,2,0:T(8,128)(2,1)} %all-gather.16.cloned.1.call-done) | copy-start | bytes 3145732
  526.5 85.0 %all-to-all-start = ((f32[16,128,2]{1,2,0:T(2,128)}), f32[16,128,2]{1,2,0:T(2,128)S(1)}, u32[]{:S(2)}, u32[]{:S(2)}) async-start(f32[16,128,2]{1,2,0:T(2,128)} %stack.2), calls=%async_computation.1 | async-start | bytes 32768 | tf_op jit(solution)/shard_map/all_to_all | solution.py:100
  536.4 75.0 %copy-start.1 = (f32[2048,2,128]{0,2,1:T(8,128)S(1)}, f32[2048,2,128]{0,2,1:T(8,128)}, u32[]{:S(2)}) copy-start(f32[2048,2,128]{0,2,1:T(8,128)} %fusion.8) | copy-start | bytes 6291460
Sparse Core Ops, SparseCore 0:
  10.0 79.1 all-gather.11
  91.3 86.0 all-gather.17
  179.9 75.2 all-gather.15
  259.2 120.6 reduce-scatter.2
  384.7 72.6 all-gather.9
  460.0 62.2 all-gather.19
  524.6 85.3 all-gather.13
  613.6 172.8 reduce-scatter.4
